TPU v7x, 32 devices: a whole 2x2x4 slice. The times are simulated.
32 devices in a mesh: grp: 4 (over x, core), dev: 8 (over z, y).
Axes of the slice: x: 2, y: 2, z: 4, core: 2. Of those that a mesh axis runs over, the one named last changes fastest.
Arguments:
- energies: bfloat16 [4096, 32768], P(('grp', 'dev')), may hold values from -48 to 48
- triples: int32 [4096, 3], P(('grp', 'dev')), may hold values from 0 to 113, as said below
- pair_surfaces: float32 [7200, 1024], P('dev'), may hold values from -24 to 24
- pair_slot: int32 [114, 114], replicated, may hold values from 0 to 7199, as said below
- single_surfaces: float32 [120, 32], P('dev'), may hold values from -12 to 12
- modals: float32 [120, 512], P('dev'), may hold values from -1 to 1
- mode_slot: int32 [114], replicated, may hold values from 0 to 119, as said below
Outputs:
- coefficients: bfloat16 [4096, 4096], P(('grp', 'dev'))
- triple_energy: float32 [4096], P(('grp', 'dev'))
- mean_field: float32 [120, 256], P('dev')
Inputs may be any that keep to these rules, and one draw needn't show every extreme that they name: The three modes of a row are distinct. Rows come in blocks of 128, one block to each device in the order of the triples' placement; all rows of a block share their first mode m, and m * (number of groups along grp) // 114 is the block's index along grp. Counting one need for each row and each of its three pairs, the rows of one block need exactly 48 surfaces from each owner along dev, the owner of pair_slot row q being q // 900. `pair_slot`: Symmetric; for two distinct modes it names the row of pair_surfaces that holds their surface, distinct pairs naming distinct rows; the diagonal is 0. `mode_slot`: distinct modes name distinct rows.
All inputs are finite; a program needn't handle non-finite values.
Results may differ from a plain program's by a relative error of at most 0.001.
Values sent between devices are 32-bit elements; how exact they have to be, the bound alone decides.
A program may use at most 128 MiB of HBM per device.

v0:
```python
import jax
import jax.numpy as jnp
from jax import lax
from jax.sharding import PartitionSpec as P

G = 32
KEEP = 16
S = 16


highest = lax.Precision.HIGHEST


def tables():
    orders = jnp.arange(KEEP, dtype=jnp.float32)
    points = jnp.arange(G, dtype=jnp.float32) + 0.5
    cosines = jnp.cos(jnp.pi * orders[:, None] * points[None, :] / G)
    weights = jnp.where(orders == 0, 1.0, 2.0) / G
    return (cosines, weights[:, None] * cosines)


def chebyshev_fit(values, fitter):
    number = values.shape[0]
    section_one = jnp.einsum(
        "cg,bgx->bcx", fitter, values.reshape(number, G, G * G), precision=highest
    )
    section_one = section_one.reshape(number, KEEP, G, G)
    section_two = jnp.einsum("dh,bchl->bcdl", fitter, section_one, precision=highest)
    return jnp.einsum("el,bcdl->bcde", fitter, section_two, precision=highest)


def oriented(picked, lower_ends, upper_ends, width):
    square = picked.reshape(-1, width, width)
    return jnp.where((lower_ends < upper_ends)[:, None, None], square, jnp.swapaxes(square, 1, 2))


def body(energies, triples, pair_surfaces, pair_slot, single_surfaces, modals, mode_slot):
    cosines, fitter = tables()
    devices = lax.axis_size("dev")
    number = triples.shape[0]
    pair_rows = pair_surfaces.shape[0]
    mode_rows = modals.shape[0]
    capacity = 3 * number // devices
    shaped = modals.reshape(mode_rows, G, S)
    local_ground = jnp.einsum("mg,cg->mc", shaped[:, :, 0] ** 2, cosines, precision=highest)
    ground, singles = (
        lax.all_gather(local_ground, "dev", axis=0, tiled=True),
        lax.all_gather(single_surfaces, "dev", axis=0, tiled=True),
    )
    lead_mode = triples[:, 0]
    second = triples[:, 1]
    third_mode = triples[:, 2]
    lower_ends = jnp.concatenate([lead_mode, lead_mode, second])
    upper_ends = jnp.concatenate([second, third_mode, third_mode])
    pair_ids = pair_slot[lower_ends, upper_ends]
    owners = pair_ids // pair_rows
    local_rows = pair_ids % pair_rows
    owner_hits = (owners[:, None] == jnp.arange(devices, dtype=jnp.int32)[None, :]).astype(
        jnp.int32
    )
    before = jnp.cumsum(owner_hits, axis=0) - owner_hits
    places = owners * capacity + jnp.sum(before * owner_hits, axis=1)
    requests = (
        jnp.zeros((devices * capacity,), jnp.int32)
        .at[places]
        .set(local_rows)
        .reshape(devices, capacity)
    )
    slot_first = mode_slot[lead_mode]
    slot_second = mode_slot[second]
    slot_third = mode_slot[third_mode]
    single_first = singles[slot_first]
    single_second = singles[slot_second]
    single_third = singles[slot_third]
    energy_block = (
        energies.astype(jnp.float32).reshape(number, G, G, G)
        - single_first[:, :, None, None]
        - single_second[:, None, :, None]
        - single_third[:, None, None, :]
    )
    wanted = lax.all_to_all(requests, "dev", split_axis=0, concat_axis=0, tiled=True)
    picked = pair_surfaces[wanted].reshape(wanted.shape + (G, G))
    reduced = jnp.einsum("cg,dh,xygh->xycd", fitter, fitter, picked, precision=highest)
    arrived = lax.all_to_all(
        reduced.reshape(wanted.shape + (KEEP * KEEP,)),
        "dev",
        split_axis=0,
        concat_axis=0,
        tiled=True,
    )
    pair_terms = oriented(
        arrived.reshape(devices * capacity, KEEP * KEEP)[places], lower_ends, upper_ends, KEEP
    )
    rowsum = jnp.sum(fitter, axis=1)
    fitted = (
        chebyshev_fit(energy_block, fitter)
        - pair_terms[:number][:, :, :, None] * rowsum[None, None, None, :]
        - pair_terms[number : 2 * number][:, :, None, :] * rowsum[None, None, :, None]
        - pair_terms[2 * number :][:, None, :, :] * rowsum[None, :, None, None]
    )
    ground_first = ground[slot_first]
    ground_second = ground[slot_second]
    ground_third = ground[slot_third]
    field_first = jnp.einsum(
        "bcde,bd,be->bc", fitted, ground_second, ground_third, precision=highest
    )
    field_second = jnp.einsum(
        "bcde,bc,be->bd", fitted, ground_first, ground_third, precision=highest
    )
    field_third = jnp.einsum(
        "bcde,bc,bd->be", fitted, ground_first, ground_second, precision=highest
    )
    triple_energy = jnp.sum(field_first * ground_first, axis=1)
    slot_ids = jnp.concatenate([slot_first, slot_second, slot_third])
    slot_range = jnp.arange(mode_rows * devices, dtype=jnp.int32)
    onehot = (slot_range[:, None] == slot_ids[None, :]).astype(jnp.float32)
    fields = jnp.concatenate([field_first, field_second, field_third], axis=0)
    partial_value = jnp.dot(onehot, fields, precision=highest)
    across = lax.psum(partial_value, "grp")
    owned = lax.psum_scatter(across, "dev", scatter_dimension=0, tiled=True)
    weighted = jnp.dot(owned, cosines, precision=highest)
    mean_field = jnp.einsum("mga,mg,mgb->mab", shaped, weighted, shaped, precision=highest).reshape(
        mode_rows, S * S
    )
    coefficients = fitted.reshape(number, KEEP * KEEP * KEEP).astype(jnp.bfloat16)
    return (coefficients, triple_energy, mean_field)


def solution(mesh):
    in_specs = (
        P(("grp", "dev"), None),
        P(("grp", "dev"), None),
        P("dev", None),
        P(),
        P("dev", None),
        P("dev", None),
        P(),
    )
    out_specs = (P(("grp", "dev"), None), P(("grp", "dev")), P("dev", None))
    return jax.shard_map(body, mesh=mesh, in_specs=in_specs, out_specs=out_specs, check_vma=False)
```

profile of v0, /device:TPU:0, one launch (start us, length us, event | category | flops | bytes accessed | tf_op | source)
XLA Modules:
  0.0 228.2 jit_solution(9718770413068440310)
XLA Ops:
  0.7 0.8 slice_bitcast_fusion
  1.5 2.8 %gather_fusion.6 = s32[384]{0:T(512)S(1)} fusion(s32[114,114]{1,0:T(8,128)S(1)} %copy-done, s32[384]{0:T(512)S(1)} %fusion.76), kind=kCustom, calls=%fused_computation.6 | custom fusion | bytes 6144 | tf_op jit(solution)/shard_map/gather | solution.py:55
  4.3 0.9 reduce-window.6
  5.2 0.2 slice_reduce_fusion
  5.6 2.9 %scatter_custom_fusion = s32[384]{0:T(512)S(1)} fusion(s32[384]{0:T(512)S(1)} %fusion.68, s32[384]{0:T(512)S(1)} %get-tuple-element.31, s32[]{:T(128)} %constant.15.clone.1), kind=kCustom, calls=%fused_computation.129 | custom fusion | bytes 1540 | tf_op jit(solution)/shard_map/scatter | solution.py:66
  8.5 0.7 all_to_all.11
  9.2 7.3 %all-to-all-start = ((s32[8,1,48]{2,1,0:T(1,128)}), s32[8,1,48]{2,1,0:T(1,128)S(1)}, u32[]{:S(2)}, u32[]{:S(2)}) async-start(s32[8,1,48]{2,1,0:T(1,128)} %all_to_all.11), calls=%async_computation | async-start | bytes 8192 | tf_op jit(solution)/shard_map/all_to_all | solution.py:81
  16.5 1.6 gather_fusion
  18.2 1.6 gather_fusion.2
  19.8 31.3 %all-gather = f32[8,15,32]{2,1,0:T(8,128)S(1)} all-gather(f32[1,15,32]{2,1,0:T(8,128)} %bitcast.110), channel_id=1, replica_groups=mesh['grp'=4,'dev'=8] {'dev'}, dimensions={0}, use_global_device_ids=true | all-gather | bytes 17280 | tf_op jit(solution)/shard_map/all_gather | solution.py:48
  51.1 0.6 gather_fusion.3
  51.7 0.6 gather_fusion.1
  52.6 0.2 convolution_bitcast_fusion.2
  52.9 30.7 %all-gather.1 = f32[8,15,16]{2,1,0:T(8,128)S(1)} all-gather(f32[1,15,16]{2,1,0:T(8,128)S(1)} %convolution_bitcast_fusion.2), channel_id=1, replica_groups=mesh['grp'=4,'dev'=8] {'dev'}, dimensions={0}, use_global_device_ids=true | all-gather | bytes 8640 | tf_op jit(solution)/shard_map/all_gather | solution.py:47
  83.6 0.6 gather_fusion.11
  84.2 0.6 gather_fusion.10
  84.9 1.2 gather_fusion.4
  86.2 0.6 gather_fusion.5
  86.8 0.6 gather_fusion.9
  88.1 15.9 %copy.88 = f32[16,8,32,1024]{3,2,1,0:T(8,128)} copy(bf16[16,8,32,1024]{3,1,2,0:T(8,128)(2,1)} %bitcast.103) | data formatting | bytes 25165824
  104.0 7.5 %fusion.2 = f32[128,32,1024]{2,1,0:T(8,128)S(1)} fusion(f32[16,8,32,1024]{3,2,1,0:T(8,128)} %copy.88, f32[128,1024]{1,0:T(8,128)S(1)} %copy.36, f32[128,1024]{1,0:T(8,128)S(1)} %copy.34, f32[128,32]{1,0:T(8,128)S(1)} %gather_fusion.1), kind=kLoop, calls=%fused_computation.15 | loop fusion | flops 12582912 | bytes 34619392 | tf_op jit(solution)/shard_map/sub | solution.py:76
  111.5 12.9 %convolution_bitcast_fusion = f32[128,16,1024]{2,1,0:T(8,128)} fusion(f32[128,32,1024]{2,1,0:T(8,128)S(1)} %fusion.2, f32[32]{0:T(128)S(1)} %iota_add_fusion, f32[16]{0:T(128)S(1)} %get-tuple-element.37, f32[16]{0:T(128)S(1)} %get-tuple-element.36), kind=kOutput, calls=%fused_computation.20 | convolution fusion | flops 805307904 | bytes 25166080 | tf_op jit(solution)/shard_map/cg,bgx->bcx/dot_general | solution.py:24
  124.4 1.7 multiply_bitcast_fusion.1
  126.2 4.8 %gather_fusion.7 = f32[384,1024]{1,0:T(8,128)S(1)} fusion(f32[900,1024]{1,0:T(8,128)} %param.9, s32[1024]{0:T(1024)S(1)} %pad_clamp_fusion.1), kind=kCustom, calls=%fused_computation.7 | custom fusion | bytes 3147264 | tf_op jit(solution)/shard_map/gather | solution.py:82
  131.0 4.2 %reshape.591 = f32[8,48,32,32]{3,2,1,0:T(8,128)} reshape(f32[384,1024]{1,0:T(8,128)S(1)} %gather_fusion.7) | data formatting | bytes 3145728 | tf_op jit(solution)/shard_map/reshape | solution.py:82
  135.2 7.6 %copy.41 = f32[8,48,32,32]{1,2,3,0:T(8,128)} copy(f32[8,48,32,32]{3,2,1,0:T(8,128)} %reshape.591) | data formatting | bytes 3145728 | tf_op jit(solution)/shard_map/reshape | solution.py:82
  142.7 4.2 %fusion.28 = f32[8,48,32,16]{1,3,2,0:T(8,128)S(1)} fusion(f32[8,48,32,32]{1,2,3,0:T(8,128)} %copy.41, f32[32]{0:T(128)S(1)} %iota_add_fusion, f32[16]{0:T(128)S(1)} %get-tuple-element.37, f32[16]{0:T(128)S(1)} %get-tuple-element.36), kind=kOutput, calls=%fused_computation.59 | convolution fusion | flops 75499008 | bytes 2359552 | tf_op jit(solution)/shard_map/cg,dh,xygh->xycd/dot_general | solution.py:83
  146.9 2.9 %fusion.10 = f32[8,48,16,16]{1,3,2,0:T(8,128)} fusion(f32[8,48,32,16]{1,3,2,0:T(8,128)S(1)} %fusion.28, f32[32]{0:T(128)S(1)} %iota_add_fusion, f32[16]{0:T(128)S(1)} %get-tuple-element.37, f32[16]{0:T(128)S(1)} %get-tuple-element.36), kind=kOutput, calls=%fused_computation.25 | convolution fusion | flops 37750272 | bytes 1179904 | tf_op jit(solution)/shard_map/cg,dh,xygh->xycd/dot_general | solution.py:83
  149.8 2.3 copy.43
  152.1 5.7 %all-to-all-start.1 = ((f32[8,48,256]{2,1,0:T(8,128)}), f32[8,48,256]{2,1,0:T(8,128)S(1)}, u32[]{:S(2)}, u32[]{:S(2)}) async-start(f32[8,48,256]{2,1,0:T(8,128)} %copy.43), calls=%async_computation.1 | async-start | bytes 786432 | tf_op jit(solution)/shard_map/all_to_all | solution.py:84
  157.9 1.6 copy.83
  159.5 0.5 copy.82
  160.0 0.5 copy.84
  160.5 8.7 %copy.37 = f32[128,16,1024]{0,2,1:T(8,128)} copy(f32[128,16,1024]{2,1,0:T(8,128)} %convolution_bitcast_fusion) | data formatting | bytes 16777216 | tf_op jit(solution)/shard_map/cg,bgx->bcx/transpose | solution.py:24
  169.2 0.6 dynamic-slice.4
  170.5 0.2 fusion.38
  170.7 13.7 %fusion.7 = f32[128,16,16,32]{0,2,3,1:T(8,128)} fusion(f32[128,16,32,32]{0,3,2,1:T(8,128)} %bitcast.101, f32[32]{0:T(128)S(1)} %iota_add_fusion, f32[16]{0:T(128)S(1)} %get-tuple-element.37, f32[16]{0:T(128)S(1)} %get-tuple-element.36), kind=kOutput, calls=%fused_computation.21 | convolution fusion | flops 402654720 | bytes 12583168 | tf_op jit(solution)/shard_map/dh,bchl->bcdl/dot_general | solution.py:28
  184.4 1.7 gather_fusion.8
  186.4 6.3 %multiply_reduce_fusion = (f32[128,16]{0,1:T(8,128)S(1)}, bf16[128,16,16,16]{0,3,2,1:T(8,128)(2,1)S(1)}, f32[128,16,16,16]{0,3,2,1:T(8,128)S(1)}) fusion(f32[128,16,16]{0,2,1:T(8,128)S(1)} %copy.84, f32[16]{0:T(128)S(1)} %fusion.38, f32[128,16,16]{0,2,1:T(8,128)S(1)} %get-tuple-element.17, f32[128,16,16]{0,2,1:T(8,128)S(1)} %get-tuple-element.18, ...), kind=kOutput, calls=%fused_computation.22 | convolution fusion | flops 206044672 | bytes 7872832 | tf_op jit(solution)/shard_map/el,bcdl->bcde/dot_general | solution.py:29
  193.1 0.2 fusion.16
  193.4 22.7 %fusion = f32[16,16]{1,0:T(8,128)S(1)} fusion(f32[120,16]{1,0:T(8,128)S(1)} %fusion.16), kind=kCustom, calls=%all-reduce-scatter | all-reduce-scatter fusion | flops 2049 | bytes 9216
  216.1 2.1 collective-permute-start
  218.2 0.6 multiply_reduce_fusion.3
  218.8 1.3 copy.54
  220.3 5.8 %psum.8 = f32[15,16]{1,0:T(8,128)S(1)} all-reduce(f32[15,16]{1,0:T(8,128)S(1)} %constant_dynamic-slice_fusion), channel_id=1, replica_groups=mesh['grp'=4,'dev'=8] {'grp'}, use_global_device_ids=true, to_apply=%region_6.7 | all-reduce | flops 240 | bytes 1920 | tf_op jit(solution)/shard_map/psum | solution.py:119
  226.0 0.2 fusion.33
  226.3 0.7 convolution_bitcast_fusion.1
  227.1 0.7 reshape.472
  (58 shorter events, 2.3 us)
Async XLA Ops:
  0.6 0.9 copy-start
  0.6 84.2 %copy-start.2 = (s32[114]{0:T(128)S(1)}, s32[114]{0:T(128)}, u32[]{:S(2)}) copy-start(s32[114]{0:T(128)} %param.13) | copy-start | bytes 1372
  0.7 51.7 %copy-start.4 = (f32[15,512]{1,0:T(8,128)S(1)}, f32[15,512]{1,0:T(8,128)}, u32[]{:S(2)}) copy-start(f32[15,512]{1,0:T(8,128)} %param.12) | copy-start | bytes 92164
  9.2 116.9 %all-to-all-start = ((s32[8,1,48]{2,1,0:T(1,128)}), s32[8,1,48]{2,1,0:T(1,128)S(1)}, u32[]{:S(2)}, u32[]{:S(2)}) async-start(s32[8,1,48]{2,1,0:T(1,128)} %all_to_all.11), calls=%async_computation | async-start | bytes 8192 | tf_op jit(solution)/shard_map/all_to_all | solution.py:81
  146.9 12.6 %copy-start.3 = (f32[128,16,16]{1,2,0:T(8,128)S(1)}, f32[128,16,16]{1,2,0:T(8,128)}, u32[]{:S(2)}) copy-start(f32[128,16,16]{1,2,0:T(8,128)} %get-tuple-element.20) | copy-start | bytes 393220
  152.1 32.2 %all-to-all-start.1 = ((f32[8,48,256]{2,1,0:T(8,128)}), f32[8,48,256]{2,1,0:T(8,128)S(1)}, u32[]{:S(2)}, u32[]{:S(2)}) async-start(f32[8,48,256]{2,1,0:T(8,128)} %copy.43), calls=%async_computation.1 | async-start | bytes 786432 | tf_op jit(solution)/shard_map/all_to_all | solution.py:84
  160.5 8.8 %copy-start.5 = (u32[32]{0:T(128)S(1)}, u32[32]{0:T(128)}, u32[]{:S(2)}) copy-start(u32[32]{0:T(128)} %constant.75) | copy-start | bytes 388
  192.7 35.1 %copy-start.1 = (s32[114,114]{1,0:T(8,128)S(1)}, s32[114,114]{1,0:T(8,128)}, u32[]{:S(2)}) copy-start(s32[114,114]{1,0:T(8,128)} %param.10) | copy-start | bytes 155956
  216.1 4.1 %collective-permute-start = (f32[7,16]{1,0:T(8,128)S(1)}, f32[7,16]{1,0:T(8,128)S(1)}, u32[]{:S(2)}, u32[]{:S(2)}) collective-permute-start(f32[7,16]{1,0:T(8,128)S(1)} %slice.65), channel_id=1, source_target_pairs={{0,1},{1,2},{2,3},{3,4},{4,5},{5,6},{6,7},{8,9},{9,10},{10,11},{11... | collective-permute-start | bytes 1352
where the time goes:
time: 232 us; the launch traced here: 228 us
  blocking collectives  90.5 us (39%)
  local copies, waits for them, and re-layouts  66.5 us (29%)
  matrix products  41.4 us (18%)
  starting transfers between devices  15.1 us (7%)
  other arithmetic  12.6 us (5%)
    all_gather x1, blocking collectives, body(): lax.all_gather(single_surfaces, 'dev', axis=0, tiled=True)  31.3 us
    all_gather x1, blocking collectives, body(): lax.all_gather(local_ground, 'dev', axis=0, tiled=True)  30.7 us
    unnamed x1, blocking collectives  22.7 us
    unnamed x23, local copies, waits for them, and re-layouts  20.5 us
    dot_general x1, matrix products, chebyshev_fit(): jnp.einsum('dh,bchl->bcdl', fitter, section_one, precision=highest)  13.7 us
    dot_general x1, matrix products, chebyshev_fit(): jnp.einsum('cg,bgx->bcx', fitter, values.reshape(number, G, G * G), preci...  12.9 us
    reshape x2, local copies, waits for them, and re-layouts, body(): picked = pair_surfaces[wanted].reshape(wanted.shape + (G, G))  11.7 us
    transpose x1, local copies, waits for them, and re-layouts, chebyshev_fit(): jnp.einsum('cg,bgx->bcx', fitter, values.reshape(number, G, G * G), preci...  8.75 us
  transfers between devices with their start and end apart: 3, of which 0 were waited for; matrix products, arithmetic and copies ran while one was open for 33% of the time, Pallas kernels for 0%

commit v1 on v0

v1 whole, which is shorter than its diff:
```python
import jax
import jax.numpy as jnp
import numpy as np
from jax import lax
from jax.experimental import pallas as pl
from jax.experimental.pallas import tpu as pltpu
from jax.sharding import PartitionSpec as P

G = 32
KEEP = 16
S = 16
PAIRS = 4

highest = lax.Precision.HIGHEST


def np_tables():
    orders = np.arange(KEEP, dtype=np.float64)
    points = np.arange(G, dtype=np.float64) + 0.5
    cosines = np.cos(np.pi * orders[:, None] * points[None, :] / G)
    weights = np.where(orders == 0, 1.0, 2.0) / G
    return cosines, weights[:, None] * cosines


COS, FIT = np_tables()
ROWSUM = FIT.astype(np.float32).sum(axis=1, dtype=np.float64)


def split(values):
    values = np.asarray(values, np.float32)
    high = values.astype(jnp.bfloat16)
    return high, (values - high.astype(np.float32)).astype(jnp.bfloat16)


PLAIN = np.einsum("dh,el->hlde", FIT, FIT).reshape(G * G, KEEP * KEEP)
SWAPPED = np.einsum("eh,dl->hlde", FIT, FIT).reshape(G * G, KEEP * KEEP)
eye = np.eye(KEEP)
SPREAD_D = np.einsum("xd,e->xde", eye, np.ones(KEEP)).reshape(KEEP, -1)
SPREAD_E = np.einsum("xe,d->xde", eye, np.ones(KEEP)).reshape(KEEP, -1)
FIRST = np.einsum("xd,e->xde", eye, ROWSUM).reshape(KEEP, -1)
SECOND = np.einsum("xe,d->xde", eye, ROWSUM).reshape(KEEP, -1)
GROUND = np.einsum("cg,s->gsc", COS, np.arange(S) == 0).reshape(G * S, KEEP)


def dot(a, b, precision=None):
    return jnp.dot(a, b, precision=precision, preferred_element_type=jnp.float32)


def pair_kernel(surf_ref, high_ref, low_ref, out_ref):
    values = surf_ref[...]
    top = values.astype(jnp.bfloat16)
    rest = (values - top.astype(jnp.float32)).astype(jnp.bfloat16)
    fitted = dot(top, high_ref[...]) + dot(top, low_ref[...]) + dot(rest, high_ref[...])
    out_ref[0] = fitted[:, : KEEP * KEEP]
    out_ref[1] = fitted[:, KEEP * KEEP :]


def pair_table(pair_surfaces):
    rows = pair_surfaces.shape[0]
    block = min(304, rows)
    steps = -(-rows // block)
    padded = steps * block
    high, low = split(np.concatenate([PLAIN, SWAPPED], axis=1))
    whole = lambda a: pl.BlockSpec(a.shape, lambda i: (0, 0))
    table = pl.pallas_call(
        pair_kernel,
        grid=(steps,),
        in_specs=[pl.BlockSpec((block, G * G), lambda i: (i, 0)), whole(high), whole(low)],
        out_specs=pl.BlockSpec((2, block, KEEP * KEEP), lambda i: (0, i, 0)),
        out_shape=jax.ShapeDtypeStruct((2, padded, KEEP * KEEP), jnp.float32),
        cost_estimate=pl.CostEstimate(
            flops=12 * rows * G * G * KEEP * KEEP, bytes_accessed=4 * rows * G * G, transcendentals=0
        ),
    )(pair_surfaces, jnp.asarray(high), jnp.asarray(low))
    return table.reshape(2 * padded, KEEP * KEEP), padded


def fit_kernel(scale_ref, front_ref, back_ref, high_ref, low_ref, acc):
    step = pl.program_id(0)
    number = front_ref.shape[0]
    high, low = high_ref[...], low_ref[...]

    @pl.when(step == 0)
    def _():
        acc[...] = jnp.zeros_like(acc)

    sums, differences = [], []
    for j in range(PAIRS):
        k = PAIRS - 1 - j
        both = jnp.concatenate(
            [front_ref[:, j * G * G : (j + 1) * G * G], back_ref[:, k * G * G : (k + 1) * G * G]],
            axis=0,
        )
        planes = dot(both, high) + dot(both, low)
        sums.append(planes[:number] + planes[number:])
        differences.append(planes[:number] - planes[number:])
    for c in range(KEEP):
        parts = sums if c % 2 == 0 else differences
        total = acc[c]
        for j in range(PAIRS):
            total += scale_ref[c, step * PAIRS + j] * parts[j]
        acc[c] = total


def field_kernel(
    acc, pair_ref, column_ref, row_ref, table_ref,
    spread_d_ref, spread_e_ref, first_ref, second_ref, expand_ref,
    coef_ref, energy_ref, partial_ref,
):
    number = acc.shape[1]
    area = KEEP * KEEP
    slots = table_ref.shape[0]
    hits = (column_ref[...] == lax.broadcasted_iota(jnp.int32, (3 * number, slots), 1))
    taken = dot(hits.astype(jnp.float32), table_ref[...], highest)
    ground, single = taken[:, :KEEP], taken[:, KEEP:]
    g1, g2, g3 = (ground[i * number : (i + 1) * number] for i in range(3))
    s1, s2, s3 = (single[i * number : (i + 1) * number] for i in range(3))
    g2e = dot(g2, spread_d_ref[...], highest)
    g3e = dot(g3, spread_e_ref[...], highest)
    weight = g2e * g3e
    p12 = pair_ref[:number] + dot(s1, first_ref[...], highest) + dot(s2, second_ref[...], highest)
    p13 = pair_ref[number : 2 * number] + dot(s3, second_ref[...], highest)
    p23 = pair_ref[2 * number :]

    def halves(values):
        top = values.astype(jnp.bfloat16).astype(jnp.float32)
        return top, values - top

    pieces = halves(p12) + halves(p13)
    lane = lax.broadcasted_iota(jnp.int32, (number, KEEP), 1)
    f1 = jnp.zeros((number, KEEP), jnp.float32)
    mixed = jnp.zeros((number, area), jnp.float32)
    for c in range(KEEP):
        left = jnp.concatenate([p[:, c * KEEP : (c + 1) * KEEP] for p in pieces], axis=1)
        correction = dot(left.astype(jnp.bfloat16), expand_ref[...])
        fitted = acc[c] - correction - p23 * float(ROWSUM[c])
        coef_ref[:, c * area : (c + 1) * area] = fitted.astype(jnp.bfloat16)
        f1 = f1 + jnp.where(lane == c, jnp.sum(fitted * weight, axis=1, keepdims=True), 0.0)
        mixed = mixed + g1[:, c : c + 1] * fitted
    gather = lambda a, b: lax.dot_general(
        a, b, (((1,), (1,)), ((), ())), precision=highest, preferred_element_type=jnp.float32
    )
    f2 = gather(mixed * g3e, spread_d_ref[...])
    f3 = gather(mixed * g2e, spread_e_ref[...])
    energy_ref[...] = jnp.sum(f1 * g1, axis=1, keepdims=True)
    fields = jnp.concatenate([f1, f2, f3], axis=0)
    hits_t = (row_ref[...] == lax.broadcasted_iota(jnp.int32, (slots, 3 * number), 0))
    partial_ref[...] = dot(hits_t.astype(jnp.float32), fields, highest)


def fit(energies):
    number = energies.shape[0]
    steps = G // 2 // PAIRS
    blocks = G // PAIRS
    high, low = split(PLAIN)
    whole = lambda a: pl.BlockSpec(a.shape, lambda i: (0, 0))
    width = PAIRS * G * G
    area = KEEP * KEEP
    return pl.pallas_call(
        fit_kernel,
        grid=(steps,),
        in_specs=[
            pl.BlockSpec(memory_space=pltpu.SMEM),
            pl.BlockSpec((number, width), lambda i: (0, i)),
            pl.BlockSpec((number, width), lambda i: (0, blocks - 1 - i)),
            whole(high),
            whole(low),
        ],
        out_specs=pl.BlockSpec((KEEP, number, area), lambda i: (0, 0, 0)),
        out_shape=jax.ShapeDtypeStruct((KEEP, number, area), jnp.float32),
        cost_estimate=pl.CostEstimate(
            flops=4 * number * G * G * G * area, bytes_accessed=2 * number * G * G * G, transcendentals=0
        ),
        compiler_params=pltpu.CompilerParams(dimension_semantics=("arbitrary",)),
    )(jnp.asarray(FIT.astype(np.float32)), energies, energies, jnp.asarray(high), jnp.asarray(low))


def fields(fitted, pair_terms, slot_ids, table):
    number = fitted.shape[1]
    first, second = FIRST.astype(np.float32), SECOND.astype(np.float32)
    spread_d, spread_e = SPREAD_D.astype(np.float32), SPREAD_E.astype(np.float32)
    expand = np.concatenate([first, first, second, second], axis=0).astype(jnp.bfloat16)
    return pl.pallas_call(
        field_kernel,
        out_shape=[
            jax.ShapeDtypeStruct((number, KEEP * KEEP * KEEP), jnp.bfloat16),
            jax.ShapeDtypeStruct((number, 1), jnp.float32),
            jax.ShapeDtypeStruct((table.shape[0], KEEP), jnp.float32),
        ],
    )(
        fitted, pair_terms, slot_ids[:, None], slot_ids[None, :], table,
        jnp.asarray(spread_d), jnp.asarray(spread_e), jnp.asarray(first), jnp.asarray(second),
        jnp.asarray(expand),
    )


def body(energies, triples, pair_surfaces, pair_slot, single_surfaces, modals, mode_slot):
    devices = lax.axis_size("dev")
    groups = lax.axis_size("grp")
    number = triples.shape[0]
    pair_rows = pair_surfaces.shape[0]
    mode_rows = modals.shape[0]
    modes = mode_slot.shape[0]
    capacity = 3 * number // devices
    cosines = jnp.asarray(COS.astype(np.float32))
    fitter = jnp.asarray(FIT.astype(np.float32))

    pairs, padded = pair_table(pair_surfaces)

    local_ground = jnp.dot(modals * modals, jnp.asarray(GROUND.astype(np.float32)), precision=highest)
    local_single = jnp.dot(single_surfaces, fitter.T, precision=highest)
    local_modes = jnp.concatenate([local_ground, local_single], axis=1).reshape(1, -1)

    a1, a2, a3 = triples[:, 0], triples[:, 1], triples[:, 2]
    lower = jnp.concatenate([a1, a1, a2])
    upper = jnp.concatenate([a2, a3, a3])
    mode_ids = jnp.arange(modes, dtype=jnp.int32)
    lines = jnp.dot(
        (lower[:, None] == mode_ids[None, :]).astype(jnp.float32),
        pair_slot.astype(jnp.float32),
        precision=highest,
    )
    pair_ids = jnp.sum(jnp.where(upper[:, None] == mode_ids[None, :], lines, 0.0), axis=1)
    pair_ids = (pair_ids + 0.5).astype(jnp.int32)
    all_modes = jnp.concatenate([a1, a2, a3])
    slot_ids = jnp.sum(
        jnp.where(all_modes[:, None] == mode_ids[None, :], mode_slot[None, :], 0), axis=1
    )
    owners = pair_ids // pair_rows
    local_rows = pair_ids - owners * pair_rows + jnp.where(lower < upper, 0, padded)
    index = jnp.arange(3 * number, dtype=jnp.int32)
    earlier = (owners[:, None] == owners[None, :]) & (index[:, None] < index[None, :])
    places = owners * capacity + jnp.sum(earlier.astype(jnp.int32), axis=0)
    requests = jnp.sum(jnp.where(places[:, None] == index[None, :], local_rows[:, None], 0), axis=0)

    sent = jnp.concatenate(
        [
            requests.astype(jnp.float32).reshape(devices, capacity),
            jnp.broadcast_to(local_modes, (devices, local_modes.shape[1])),
        ],
        axis=1,
    )
    received = lax.all_to_all(sent, "dev", split_axis=0, concat_axis=0, tiled=True)
    wanted = received[:, :capacity].astype(jnp.int32).reshape(-1)
    table = received[:, capacity:].reshape(devices * mode_rows, 2 * KEEP)
    answers = pairs[wanted].reshape(devices, capacity, KEEP * KEEP)
    arrived = lax.all_to_all(answers, "dev", split_axis=0, concat_axis=0, tiled=True)
    pair_terms = arrived.reshape(devices * capacity, KEEP * KEEP)[places]

    coefficients, energy, partial = fields(fit(energies), pair_terms, slot_ids, table)

    spread = jnp.broadcast_to(
        partial.reshape(1, devices, mode_rows, KEEP), (groups, devices, mode_rows, KEEP)
    ).reshape(groups * devices, mode_rows, KEEP)
    moments = jnp.sum(
        lax.all_to_all(spread, ("grp", "dev"), split_axis=0, concat_axis=0, tiled=True), axis=0
    )
    weighted = jnp.dot(moments, cosines, precision=highest)
    shaped = modals.reshape(mode_rows, G, S)
    mean_field = jnp.einsum("mga,mg,mgb->mab", shaped, weighted, shaped, precision=highest)
    return coefficients, energy.reshape(number), mean_field.reshape(mode_rows, S * S)


def solution(mesh):
    in_specs = (
        P(("grp", "dev"), None),
        P(("grp", "dev"), None),
        P("dev", None),
        P(),
        P("dev", None),
        P("dev", None),
        P(),
    )
    out_specs = (P(("grp", "dev"), None), P(("grp", "dev")), P("dev", None))
    return jax.shard_map(body, mesh=mesh, in_specs=in_specs, out_specs=out_specs, check_vma=False)
```

time: 232 us -> 69.7 us (0.30); the launches traced: 228 us -> 69 us
  blocking collectives: 90.5 us -> 0 us
  local copies, waits for them, and re-layouts: 66.5 us -> 13.1 us
  matrix products: 41.4 us -> 4.09 us
  Pallas kernels: 0 us -> 23.3 us
  other arithmetic: 12.6 us -> 2.85 us
  waiting for transfers between devices: 0.01 us -> 5.66 us
  starting transfers between devices: 15.1 us -> 19.2 us
    all_gather x2 -> x0, blocking collectives: 62 us -> none  [the longest x1 31.3 us: body(): lax.all_gather(single_surfaces, 'dev', axis=0, tiled=True)]
    dot_general x8 -> x4, matrix products: 40.7 us -> 3.4 us  [the longest x1 1.22 us: body(): jnp.dot((lower[:, None] == mode_ids[None, :]).astype(jnp.float32), pair_s...]
    pallas_call x0 -> x3, Pallas kernels: none -> 23.3 us  [the longest x1 11.5 us: fit(): pl.pallas_call(fit_kernel, grid=(steps,), in_specs=[pl.BlockSpec(memory_s...]
    unnamed x1 -> x0, blocking collectives: 22.7 us -> none
    unnamed x23 -> x11, local copies, waits for them, and re-layouts: 20.5 us -> 0.9 us
    reshape x4 -> x5, local copies, waits for them, and re-layouts: 14.7 us -> 1.66 us  [the longest x1 0.72 us: body(): mean_field.reshape(mode_rows, S * S)]
    gather x15 -> x2, local copies, waits for them, and re-layouts: 17.8 us -> 5.87 us  [the longest x1 3.7 us: body(): answers = pairs[wanted].reshape(devices, capacity, KEEP * KEEP)]
    transpose x1 -> x0, local copies, waits for them, and re-layouts: 8.75 us -> none  [chebyshev_fit(): jnp.einsum('cg,bgx->bcx', fitter, values.reshape(number, G, G * G), preci...]
  transfers between devices with their start and end apart: 3 -> 3, of which waited for: 0 -> 2; matrix products, arithmetic and copies ran while one was open for 33% -> 6% of each run, Pallas kernels for 0% -> 26%
where the time goes in v1:
time: 69.7 us; the launch traced here: 69 us
  Pallas kernels  23.3 us (33%)
  starting transfers between devices  19.2 us (28%)
  local copies, waits for them, and re-layouts  13.1 us (19%)
  waiting for transfers between devices  5.66 us (8%)
  matrix products  4.09 us (6%)
  other arithmetic  2.85 us (4%)
  between operations  0.78 us (1%)
    pallas_call x1, Pallas kernels, fit(): pl.pallas_call(fit_kernel, grid=(steps,), in_specs=[pl.BlockSpec(memory_s...  11.5 us
    all_to_all x1, starting transfers between devices, body(): lax.all_to_all(sent, 'dev', split_axis=0, concat_axis=0, tiled=True)  7.31 us
    pallas_call x1, Pallas kernels, pair_table(): pl.pallas_call(pair_kernel, grid=(steps,), in_specs=[pl.BlockSpec((block,...  6.53 us
    all_to_all x1, starting transfers between devices, body(): lax.all_to_all(spread, ('grp', 'dev'), split_axis=0, concat_axis=0, tiled...  6 us
    all_to_all x1, starting transfers between devices, body(): lax.all_to_all(answers, 'dev', split_axis=0, concat_axis=0, tiled=True)  5.92 us
    all_to_all x1, waiting for transfers between devices, body(): lax.all_to_all(spread, ('grp', 'dev'), split_axis=0, concat_axis=0, tiled...  5.58 us
    pallas_call x1, Pallas kernels, fields(): pl.pallas_call(field_kernel, out_shape=[jax.ShapeDtypeStruct((number, KEE...  5.3 us
    gather x1, local copies, waits for them, and re-layouts, body(): answers = pairs[wanted].reshape(devices, capacity, KEEP * KEEP)  3.7 us
  transfers between devices with their start and end apart: 3, of which 2 were waited for; matrix products, arithmetic and copies ran while one was open for 6% of the time, Pallas kernels for 26%

profile of v1, /device:TPU:0, one launch (start us, length us, event | category | flops | bytes accessed | tf_op | source)
XLA Modules:
  0.0 69.0 jit_solution(17669000749375282564)
XLA Ops:
  0.6 0.0 copy-start
  0.6 0.8 %slice_bitcast_fusion.1 = (s32[128]{0:T(128)S(1)}, s32[128]{0:T(128)S(1)}, s32[128]{0:T(128)S(1)}) fusion(s32[128,3]{0,1:T(4,128)} %param.21), kind=kLoop, calls=%fused_computation.48 | loop fusion | bytes 3072 | tf_op jit(solution)/shard_map/squeeze | solution.py:214
  1.5 1.2 %fusion = f32[384]{0:T(512)S(1)} fusion(s32[384]{0:T(512)S(1)} %get-tuple-element.18, s32[384]{0:T(512)S(1)} %get-tuple-element.17, s32[114,114]{1,0:T(8,128)} %param.23), kind=kOutput, calls=%fused_computation.4 | convolution fusion | flops 60073284 | bytes 56592 | tf_op jit(solution)/shard_map/dot_general | solution.py:218
  2.7 0.1 convert_reduce_fusion
  2.9 0.2 select_reduce_fusion
  3.0 0.1 convert_element_type.45
  3.1 0.0 copy-done
  3.1 0.8 %convolution_bitcast_fusion.1 = f32[15,16]{1,0:T(8,128)S(1)} fusion(f32[16,32]{1,0:T(8,128)} %constant.51.clone.scale_ref, f32[15,32]{1,0:T(8,128)S(1)} %copy-done), kind=kOutput, calls=%fused_computation.5 | convolution fusion | flops 92160 | bytes 4928 | tf_op jit(solution)/shard_map/dot_general | solution.py:211
  4.0 1.2 %fusion.6 = f32[15,16]{1,0:T(8,128)S(1)} fusion(f32[512,16]{1,0:T(8,128)} %constant.54.clone, f32[15,512]{1,0:T(8,128)} %param.25), kind=kOutput, calls=%fused_computation.20 | convolution fusion | flops 1482240 | bytes 64448 | tf_op jit(solution)/shard_map/dot_general | solution.py:210
  5.2 0.1 pad_maximum_fusion.1
  5.3 0.1 reshape.236
  5.3 0.1 pad.4.clone
  5.4 0.6 all_to_all.14
  6.1 7.3 %all-to-all-start = ((f32[8,1,528]{2,1,0:T(1,128)}), f32[8,1,528]{2,1,0:T(1,128)S(1)}, u32[]{:S(2)}, u32[]{:S(2)}) async-start(f32[8,1,528]{2,1,0:T(1,128)} %all_to_all.14), calls=%async_computation | async-start | bytes 40960 | tf_op jit(solution)/shard_map/all_to_all | solution.py:243
  13.4 6.5 %shard_map.212 = f32[2,912,256]{2,1,0:T(8,128)} custom-call(f32[900,1024]{1,0:T(8,128)} %surf_ref.1, bf16[1024,512]{1,0:T(8,128)(2,1)} %constant.52.clone.high_ref, bf16[1024,512]{1,0:T(8,128)(2,1)} %constant.53.clone.low_ref), custom_call_target="tpu_custom_call" | custom-call | flops 2831155200 | bytes 3686400 | tf_op jit(solution)/shard_map/pallas_call | solution.py:65
  19.9 0.1 all-to-all-done
  20.0 0.1 reshape.207
  20.1 0.0 copy-start.3
  20.1 3.7 %gather_fusion = f32[384,256]{1,0:T(8,128)} fusion(f32[1824,256]{1,0:T(8,128)} %bitcast.25, s32[1024]{0:T(1024)S(1)} %pad_clamp_fusion.1), kind=kCustom, calls=%fused_computation | custom fusion | bytes 787968 | tf_op jit(solution)/shard_map/gather | solution.py:246
  23.8 5.9 %all-to-all-start.1 = ((f32[8,48,256]{2,1,0:T(8,128)}), f32[8,48,256]{2,1,0:T(8,128)S(1)}, u32[]{:S(2)}, u32[]{:S(2)}) async-start(f32[8,48,256]{2,1,0:T(8,128)} %bitcast.5), calls=%async_computation.1 | async-start | bytes 786432 | tf_op jit(solution)/shard_map/all_to_all | solution.py:247
  29.7 0.0 copy-done.3
  29.7 0.1 select_reduce_fusion.1
  29.8 0.8 %broadcast_in_dim.82.column_ref = s32[384,1]{1,0:T(8,128)} reshape(s32[384]{0:T(512)S(1)} %select_reduce_fusion.1) | data formatting | bytes 3072 | tf_op jit(solution)/shard_map/broadcast_in_dim | solution.py:191
  30.6 0.6 broadcast_in_dim.79.row_ref
  31.2 11.5 %shard_map.211.acc = f32[16,128,256]{2,1,0:T(8,128)} custom-call(f32[16,32]{1,0:T(8,128)} %constant.51.clone.scale_ref, bf16[128,32768]{1,0:T(8,128)(2,1)} %back_ref.1, bf16[128,32768]{1,0:T(8,128)(2,1)} %back_ref.1, bf16[1024,256]{1,0:T(8,128)(2,1)} %constant.55.clone.high_ref, bf16[1024,256]{1,0:T(8,128)(2,1)} %constant.56.clone.low_ref), custom_call_target="tpu_custom_call" | custom-call | flops 4294967296 | bytes 8388608 | tf_op jit(solution)/shard_map/pallas_call | solution.py:159
  42.7 0.1 slice.25
  42.8 0.7 %reshape.210.table_ref = f32[120,32]{1,0:T(8,128)} reshape(f32[8,480]{1,0:T(8,128)S(1)} %slice.25) | data formatting | bytes 30720 | tf_op jit(solution)/shard_map/reshape | solution.py:245
  43.5 0.0 all-to-all-done.1
  43.5 2.2 %gather_fusion.1 = f32[384,256]{1,0:T(8,128)} fusion(f32[384,256]{1,0:T(8,128)S(1)} %bitcast.24, s32[1024]{0:T(1024)S(1)} %pad_clamp_fusion), kind=kCustom, calls=%fused_computation.1 | custom fusion | bytes 787968 | tf_op jit(solution)/shard_map/gather | solution.py:248
  45.7 0.0 copy-start.1
  45.7 0.0 copy-start.2
  45.7 5.3 %shard_map.213 = (bf16[128,4096]{1,0:T(8,128)(2,1)}, f32[128,1]{1,0:T(8,128)}, f32[120,16]{1,0:T(8,128)}) custom-call(f32[16,128,256]{2,1,0:T(8,128)} %shard_map.211.acc, f32[384,256]{1,0:T(8,128)} %gather_fusion.1, s32[384,1]{1,0:T(8,128)} %broadcast_in_dim.82.column_ref, s32[1,384]{1,0:T(1,128)} %broadcast_in_dim.79.row_ref, ...), custom_call_target="tpu_custom_call" | custom-call | tf_op jit(solution)/shard_map/pallas_call | solution.py:183
  51.0 0.8 %reshape.232 = f32[8,15,16]{2,1,0:T(8,128)S(1)} reshape(f32[120,16]{1,0:T(8,128)} %get-tuple-element.8) | data formatting | bytes 15360 | tf_op jit(solution)/shard_map/broadcast_in_dim | solution.py:252
  51.9 0.1 copy.53
  52.0 0.8 %reshape.244 = f32[32,1,240]{2,1,0:T(1,128)} reshape(f32[32,15,16]{2,1,0:T(8,128)S(1)} %copy.53) | data formatting | bytes 61440
  52.8 6.0 %all-to-all-start.2 = ((f32[32,1,240]{2,1,0:T(1,128)}), f32[32,1,240]{2,1,0:T(1,128)S(1)}, u32[]{:S(2)}, u32[]{:S(2)}) async-start(f32[32,1,240]{2,1,0:T(1,128)} %reshape.244), calls=%async_computation.2 | async-start | bytes 65536 | tf_op jit(solution)/shard_map/all_to_all | solution.py:256
  58.8 0.0 copy-done.1
  58.8 0.1 reshape.213
  58.9 1.5 %reduce.2 = f32[128]{0:T(128)} reduce(f32[128,1]{1,0:T(8,128)} %get-tuple-element.7, f32[]{:T(128)} %constant.67), dimensions={1}, to_apply=%get-tuple-element.7.reduce_sub_computation | reduce | bytes 1028 | tf_op jit(solution)/shard_map/pallas_call | solution.py:183
  60.4 5.6 %all-to-all-done.2 = f32[32,1,240]{2,1,0:T(1,128)S(1)} async-done(((f32[32,1,240]{2,1,0:T(1,128)}), f32[32,1,240]{2,1,0:T(1,128)S(1)}, u32[]{:S(2)}, u32[]{:S(2)}) %all-to-all-start.2) | async-done | bytes 30752 | tf_op jit(solution)/shard_map/all_to_all | solution.py:256
  66.0 0.5 broadcast.199
  66.5 0.7 %reduce.5 = f32[32,240]{1,0:T(8,128)S(1)} reduce(f32[32,1,240]{2,1,0:T(1,128)S(1)} %all-to-all-done.2, f32[]{:T(128)} %broadcast.199), dimensions={1}, to_apply=%all_to_all.18.reduce_sub_computation | reduce | bytes 61444 | tf_op jit(solution)/shard_map/all_to_all | solution.py:256
  67.2 0.1 reshape.245
  67.4 0.0 copy-done.2
  67.4 0.1 fusion.15
  67.5 0.7 convolution_bitcast_fusion
  68.2 0.1 copy.57
  68.3 0.7 %reshape.214 = f32[15,256]{1,0:T(8,128)} reshape(f32[15,16,16]{2,1,0:T(8,128)S(1)} %copy.57) | data formatting | bytes 30720 | tf_op jit(solution)/shard_map/reshape | solution.py:261
  (14 shorter events, 0.2 us)
Async XLA Ops:
  0.6 2.5 %copy-start = (f32[15,32]{1,0:T(8,128)S(1)}, f32[15,32]{1,0:T(8,128)}, u32[]{:S(2)}) copy-start(f32[15,32]{1,0:T(8,128)} %param.24) | copy-start | bytes 5764
  6.1 13.9 %all-to-all-start = ((f32[8,1,528]{2,1,0:T(1,128)}), f32[8,1,528]{2,1,0:T(1,128)S(1)}, u32[]{:S(2)}, u32[]{:S(2)}) async-start(f32[8,1,528]{2,1,0:T(1,128)} %all_to_all.14), calls=%async_computation | async-start | bytes 40960 | tf_op jit(solution)/shard_map/all_to_all | solution.py:243
  20.1 9.6 %copy-start.3 = (s32[114]{0:T(128)S(1)}, s32[114]{0:T(128)}, u32[]{:S(2)}) copy-start(s32[114]{0:T(128)} %param.26) | copy-start | bytes 1372
  23.8 19.7 %all-to-all-start.1 = ((f32[8,48,256]{2,1,0:T(8,128)}), f32[8,48,256]{2,1,0:T(8,128)S(1)}, u32[]{:S(2)}, u32[]{:S(2)}) async-start(f32[8,48,256]{2,1,0:T(8,128)} %bitcast.5), calls=%async_computation.1 | async-start | bytes 786432 | tf_op jit(solution)/shard_map/all_to_all | solution.py:247
  45.7 13.1 %copy-start.1 = (f32[15,512]{1,0:T(8,128)S(1)}, f32[15,512]{1,0:T(8,128)}, u32[]{:S(2)}) copy-start(f32[15,512]{1,0:T(8,128)} %param.25) | copy-start | bytes 92164
  45.7 21.7 %copy-start.2 = (f32[16,32]{1,0:T(8,128)S(1)}, f32[16,32]{1,0:T(8,128)}, u32[]{:S(2)}) copy-start(f32[16,32]{1,0:T(8,128)} %constant.50.clone) | copy-start | bytes 6148
  52.8 13.2 %all-to-all-start.2 = ((f32[32,1,240]{2,1,0:T(1,128)}), f32[32,1,240]{2,1,0:T(1,128)S(1)}, u32[]{:S(2)}, u32[]{:S(2)}) async-start(f32[32,1,240]{2,1,0:T(1,128)} %reshape.244), calls=%async_computation.2 | async-start | bytes 65536 | tf_op jit(solution)/shard_map/all_to_all | solution.py:256
